TPU v7x, 32 devices: a whole 2x2x4 slice. The times are simulated.
32 devices in a mesh: inst: 16 (over z, y, x), cells: 2 (over core).
Axes of the slice: x: 2, y: 2, z: 4, core: 2. Of those that a mesh axis runs over, the one named last changes fastest.
Arguments:
- adjoint: float32 [16, 5, 8, 16, 128], P('inst', None, 'cells'), may hold values from -6 to 6
- objective_gradient: float32 [16, 5, 8, 16, 128], P('inst', None, 'cells'), may hold values from -6 to 6
- jacobian: float32 [16, 3, 5, 5, 8, 16, 128], P('inst', None, None, None, 'cells'), may hold values from -2.5 to 2.5
- second_coef: float32 [16, 3, 8, 16, 128], P('inst', None, 'cells'), may hold values from 0.05 to 0.5
- fourth_coef: float32 [16, 3, 8, 16, 128], P('inst', None, 'cells'), may hold values from 0.01 to 0.1
- time_step: float32 [16, 8, 16, 128], P('inst', 'cells'), may hold values from 0.03 to 0.15
- frequency: float32 [1], replicated, may hold values from 0.5 to 1.5
- damping: float32 [1], replicated, may hold values from 0.02 to 0.08
Outputs:
- updated: float32 [16, 5, 8, 16, 128], P('inst', None, 'cells')
All inputs are finite; a program needn't handle non-finite values.
Results may differ from a plain program's by a relative error of at most 0.0001.
Values sent between devices are 32-bit elements; how exact they have to be, the bound alone decides.
A program may use at most 64 MiB of HBM per device.

v0:
```python
import functools
import math

import jax
import jax.numpy as jnp
from jax import lax
from jax.experimental import pallas as pl
from jax.experimental.pallas import tpu as pltpu
from jax.sharding import PartitionSpec as P

FACTORS = (0.25, 1.0 / 6.0, 0.375, 0.5, 1.0)
PAD = 8
MESH = pl.DeviceIdType.MESH

A_OUT, A_MIX, V1_OUT, U1_OUT, V2_BACK, V2_MIX, V3_OUT, U3_OUT, V4_BACK, V4_MIX = range(10)
UNITS = 10


def coupling_tables(count):
    slope, curve = [0.0], [count * count / 12.0 + 1.0 / 6.0]
    for m in range(1, count):
        parity = 1.0 if m % 2 == 0 else -1.0
        angle = math.pi * m / count
        slope.append(0.5 * parity * math.cos(angle) / math.sin(angle))
        curve.append(0.5 * parity / math.sin(angle) ** 2)
    return slope, curve


def kernel(
    n, cells, adj, grad, jac, c2, c4, dt, freq_in, damp_in, out,
    vp, jv, cx, cy, cz, kk, dtv, gv, zz, sx, rx, mm, sdt, rdt, coef, freq, damp,
    loc_sem, ss, rs, dss, drs, hss, hrs, chs, chr_,
):
    nv, lay, ny, nz = adj.shape
    rows = lay * ny // n
    per = ny // rows
    me = lax.axis_index("inst")
    cell = lax.axis_index("cells")
    has_lo = cell > 0
    has_hi = cell < cells - 1
    mid = slice(PAD, PAD + ny)

    local = [
        (adj, vp.at[0, :, 2 : 2 + lay, mid, :]),
        (dt, dtv),
        (c2.at[0], cx.at[0, 2 : 2 + lay]),
        (c4.at[0], cx.at[1, 2 : 2 + lay]),
        (c2.at[1], cy.at[0, :, mid, :]),
        (c4.at[1], cy.at[1, :, mid, :]),
        (c2.at[2], cz.at[0]),
        (c4.at[2], cz.at[1]),
        (grad, gv),
        (jac, jv),
        (freq_in, freq),
        (damp_in, damp),
    ]
    local = [pltpu.make_async_copy(s, d, loc_sem.at[i]) for i, (s, d) in enumerate(local)]
    for c in local:
        c.start()

    barrier = pltpu.get_barrier_semaphore()

    @pl.loop(1, n)
    def _(r):
        pl.semaphore_signal(
            barrier, inc=1, device_id={"inst": lax.rem(me + r, n)}, device_id_type=MESH
        )

    @pl.when(has_lo)
    def _():
        pl.semaphore_signal(barrier, inc=1, device_id={"cells": cell - 1}, device_id_type=MESH)

    @pl.when(has_hi)
    def _():
        pl.semaphore_signal(barrier, inc=1, device_id={"cells": cell + 1}, device_id_type=MESH)

    slope, curve = coupling_tables(n)
    local[10].wait()
    local[11].wait()
    for m in range(n):
        value = freq[0] * slope[m] + damp[0] * curve[m]
        coef[m] = value
        coef[m + n] = value
    pads = jnp.zeros((nv, lay, PAD, nz), jnp.float32)
    for s in range(len(FACTORS)):
        vp[s, :, 2 : 2 + lay, 0:PAD, :] = pads
        vp[s, :, 2 : 2 + lay, PAD + ny :, :] = pads
    cy[:, :, 0:PAD, :] = jnp.zeros((2, lay, PAD, nz), jnp.float32)
    cy[:, :, PAD + ny :, :] = jnp.zeros((2, lay, PAD, nz), jnp.float32)

    @pl.when(jnp.logical_not(has_lo))
    def _():
        cx[:, 0:2] = jnp.zeros((2, 2, ny, nz), jnp.float32)
        for s in range(len(FACTORS)):
            vp[s, :, 0:2, mid, :] = jnp.zeros((nv, 2, ny, nz), jnp.float32)

    @pl.when(jnp.logical_not(has_hi))
    def _():
        cx[:, 2 + lay :] = jnp.zeros((2, 2, ny, nz), jnp.float32)
        for s in range(len(FACTORS)):
            vp[s, :, 2 + lay :, mid, :] = jnp.zeros((nv, 2, ny, nz), jnp.float32)

    half = n // 2

    def partner(i):
        own = i // half
        return lax.rem(me // half + 1 + own, 2) * half + lax.rem(
            lax.rem(me, half) + i + own, half
        )

    def chunk(unit, p, slot):
        return pltpu.make_async_remote_copy(
            src_ref=sx.at[unit, p], dst_ref=rx.at[unit, slot],
            send_sem=ss.at[unit, p], recv_sem=rs.at[unit, slot],
            device_id={"inst": p}, device_id_type=MESH,
        )

    def send(unit):
        @pl.loop(0, n - 1)
        def _(i):
            chunk(unit, partner(i), me).start()

        rx[unit, me] = sx[unit, me]

    def receive(unit):
        @pl.loop(1, n)
        def _(r):
            p = lax.rem(me + r, n)
            chunk(unit, p, p).wait_recv()

    def dt_chunk(p, slot):
        return pltpu.make_async_remote_copy(
            src_ref=sdt.at[p], dst_ref=rdt.at[slot],
            send_sem=dss.at[p], recv_sem=drs.at[slot],
            device_id={"inst": p}, device_id_type=MESH,
        )

    def halo_up(s):
        return pltpu.make_async_remote_copy(
            src_ref=vp.at[s, :, lay : lay + 2, mid, :], dst_ref=vp.at[s, :, 0:2, mid, :],
            send_sem=hss.at[s, 0], recv_sem=hrs.at[s, 0],
            device_id={"cells": cell + 1}, device_id_type=MESH,
        )

    def halo_down(s):
        return pltpu.make_async_remote_copy(
            src_ref=vp.at[s, :, 2:4, mid, :], dst_ref=vp.at[s, :, 2 + lay : 4 + lay, mid, :],
            send_sem=hss.at[s, 1], recv_sem=hrs.at[s, 1],
            device_id={"cells": cell - 1}, device_id_type=MESH,
        )

    coef_up = pltpu.make_async_remote_copy(
        src_ref=cx.at[:, lay : lay + 2], dst_ref=cx.at[:, 0:2],
        send_sem=chs.at[0], recv_sem=chr_.at[0],
        device_id={"cells": cell + 1}, device_id_type=MESH,
    )
    coef_down = pltpu.make_async_remote_copy(
        src_ref=cx.at[:, 2:4], dst_ref=cx.at[:, 2 + lay : 4 + lay],
        send_sem=chs.at[1], recv_sem=chr_.at[1],
        device_id={"cells": cell - 1}, device_id_type=MESH,
    )

    def start_pair(up, down):
        @pl.when(has_hi)
        def _():
            up.start()

        @pl.when(has_lo)
        def _():
            down.start()

    def land_pair(up, down):
        @pl.when(has_lo)
        def _():
            up.wait_recv()

        @pl.when(has_hi)
        def _():
            down.wait_recv()

    def sent_pair(up, down):
        @pl.when(has_hi)
        def _():
            up.wait_send()

        @pl.when(has_lo)
        def _():
            down.wait_send()

    def pieces(body):
        @pl.loop(0, lay)
        def _(x):
            for q in range(per):
                for b in range(nv):
                    body(
                        x, x * per + q, b, slice(b * rows, (b + 1) * rows),
                        slice(q * rows, (q + 1) * rows),
                        slice(PAD + q * rows, PAD + (q + 1) * rows),
                    )

    def pack(s, unit):
        def body(x, d, b, chunk_rows, plain, padded):
            sx[unit, d, chunk_rows, :] = vp[s, b, 2 + x, padded, :]

        pieces(body)

    def unpack(unit, s):
        def body(x, d, b, chunk_rows, plain, padded):
            vp[s, b, 2 + x, padded, :] = rx[unit, d, chunk_rows, :]

        pieces(body)

    def finish(unit, s):
        factor = FACTORS[s - 1]

        def body(x, d, b, chunk_rows, plain, padded):
            vp[s, b, 2 + x, padded, :] = zz[b, x, plain, :] - (factor * dtv[x, plain, :]) * rx[
                unit, d, chunk_rows, :
            ]

        pieces(body)

    lanes = lax.broadcasted_iota(jnp.int32, (ny, nz), 1)
    half_lo = jnp.where(lanes >= 1, 0.5, 0.0)
    half_hi = jnp.where(lanes < nz - 1, 0.5, 0.0)

    def stencil():
        @pl.loop(0, lay)
        def _(x):
            up4 = cx[1, x + 3]
            here3 = 3.0 * cx[1, x + 2] + cx[0, x + 2]
            below3 = 3.0 * cx[1, x + 1] + cx[0, x + 1]
            below4 = cx[1, x]
            kk[0, x] = below4
            kk[1, x] = -(below3 + below4)
            kk[2, x] = -(up4 + here3)
            kk[3, x] = up4
            centre = here3 + below3
            up4 = cy[1, x, PAD + 1 : PAD + 1 + ny, :]
            here3 = 3.0 * cy[1, x, mid, :] + cy[0, x, mid, :]
            low = slice(PAD - 1, PAD - 1 + ny)
            below3 = 3.0 * cy[1, x, low, :] + cy[0, x, low, :]
            below4 = cy[1, x, PAD - 2 : PAD - 2 + ny, :]
            kk[4, x] = below4
            kk[5, x] = -(below3 + below4)
            kk[6, x] = -(up4 + here3)
            kk[7, x] = up4
            centre = centre + here3 + below3
            here4 = cz[1, x]
            here3 = 3.0 * here4 + cz[0, x]
            up4 = jnp.where(lanes < nz - 1, pltpu.roll(here4, nz - 1, 1), 0.0)
            below3 = jnp.where(lanes >= 1, pltpu.roll(here3, 1, 1), 0.0)
            below4 = jnp.where(lanes >= 2, pltpu.roll(here4, 2, 1), 0.0)
            kk[8, x] = below4
            kk[9, x] = jnp.where(lanes >= 1, -(below3 + below4), 0.0)
            kk[10, x] = jnp.where(lanes < nz - 1, -(up4 + here3), 0.0)
            kk[11, x] = jnp.where(lanes < nz - 2, up4, 0.0)
            kk[12, x] = centre + here3 + below3

    def spatial(s, emit):
        factor = FACTORS[s]
        both = has_lo.astype(jnp.int32) * has_hi.astype(jnp.int32)
        back = has_lo.astype(jnp.int32) * (1 - both)
        late = (lay - 2) * (1 - both)

        @pl.loop(0, lay)
        def _(i):
            @pl.when(i == late)
            def _():
                land_pair(halo_up(s), halo_down(s))

            x = back * (lay - 1 - i) + (1 - back) * i
            sums, central = [], [[], [], []]
            for b in range(nv):
                v0 = vp[s, b, x + 2, mid, :]
                total = kk[12, x] * v0
                m2, m1 = vp[s, b, x, mid, :], vp[s, b, x + 1, mid, :]
                p1, p2 = vp[s, b, x + 3, mid, :], vp[s, b, x + 4, mid, :]
                total += kk[0, x] * m2 + kk[1, x] * m1 + kk[2, x] * p1 + kk[3, x] * p2
                central[0].append(0.5 * (m1 - p1))
                m2, m1, p1, p2 = (
                    vp[s, b, x + 2, PAD + o : PAD + o + ny, :] for o in (-2, -1, 1, 2)
                )
                total += kk[4, x] * m2 + kk[5, x] * m1 + kk[6, x] * p1 + kk[7, x] * p2
                central[1].append(0.5 * (m1 - p1))
                m2, m1, p1, p2 = (pltpu.roll(v0, o, 1) for o in (2, 1, nz - 1, nz - 2))
                total += kk[8, x] * m2 + kk[9, x] * m1 + kk[10, x] * p1 + kk[11, x] * p2
                central[2].append(half_lo * m1 - half_hi * p1)
                sums.append(total)
            step = factor * dtv[x]
            for b in range(nv):
                total = sums[b] + gv[b, x]
                for d in range(3):
                    for a in range(nv):
                        total += jv[d, a, b, x] * central[d][a]
                emit(x, b, vp[0, b, x + 2, mid, :] - step * total)

    def to_home(x, b, value):
        zz[b, x] = value

    def to_chunks(unit):
        def emit(x, b, value):
            for q in range(per):
                sx[unit, x * per + q, b * rows : (b + 1) * rows, :] = value[
                    q * rows : (q + 1) * rows
                ]

        return emit

    def mixed(source, k):
        total = coef[n - k] * source(0)
        for j in range(1, n):
            total += coef[n + j - k] * source(j)
        return total

    def form_and_send(unit, form):
        @pl.loop(0, n - 1)
        def _(i):
            p = partner(i)
            sx[unit, p] = form(p)

            @pl.when(i > 0)
            def _():
                chunk(unit, partner(i - 1), me).start()

        value = form(me)
        sx[unit, me] = value
        rx[unit, me] = value
        chunk(unit, partner(n - 2), me).start()

    local[0].wait()
    pack(0, A_OUT)
    pl.semaphore_wait(barrier, n - 1 + has_lo.astype(jnp.int32) + has_hi.astype(jnp.int32))
    send(A_OUT)
    start_pair(halo_up(0), halo_down(0))
    local[2].wait()
    local[3].wait()
    start_pair(coef_up, coef_down)
    local[1].wait()

    @pl.loop(0, lay)
    def _(x):
        for q in range(per):
            sdt[x * per + q] = dtv[x, q * rows : (q + 1) * rows, :]

    @pl.loop(1, n)
    def _(r):
        dt_chunk(lax.rem(me + r, n), me).start()

    rdt[me] = sdt[me]
    for c in local[4:10]:
        c.wait()
    land_pair(coef_up, coef_down)
    stencil()
    spatial(0, to_home)
    receive(A_OUT)

    form_and_send(A_MIX, lambda k: mixed(lambda j: rx[A_OUT, j], k))

    @pl.loop(1, n)
    def _(r):
        p = lax.rem(me + r, n)
        dt_chunk(p, p).wait_recv()

    receive(A_MIX)
    finish(A_MIX, 1)

    for s, v_out, u_out, v_back, v_mix in (
        (1, V1_OUT, U1_OUT, V2_BACK, V2_MIX),
        (3, V3_OUT, U3_OUT, V4_BACK, V4_MIX),
    ):
        start_pair(halo_up(s), halo_down(s))
        pack(s, v_out)
        send(v_out)
        spatial(s, to_chunks(u_out))
        send(u_out)
        receive(v_out)

        @pl.loop(0, n)
        def _(k):
            mm[k] = mixed(lambda j: rx[v_out, j], k)

        def advance(k, s=s, u_out=u_out):
            @pl.when(k != me)
            def _():
                chunk(u_out, k, k).wait_recv()

            step = FACTORS[s] * rdt[k]
            return rx[u_out, k] - jnp.concatenate([step] * nv, axis=0) * mm[k]

        form_and_send(v_back, advance)
        form_and_send(v_mix, lambda k: mixed(lambda j: sx[v_back, j], k))
        receive(v_back)
        unpack(v_back, s + 1)
        start_pair(halo_up(s + 1), halo_down(s + 1))
        spatial(s + 1, to_home)
        receive(v_mix)
        if s + 2 < len(FACTORS):
            finish(v_mix, s + 2)

    def last(x, d, b, chunk_rows, plain, padded):
        out[b, x, plain, :] = zz[b, x, plain, :] - (FACTORS[-1] * dtv[x, plain, :]) * rx[
            V4_MIX, d, chunk_rows, :
        ]

    pieces(last)

    @pl.loop(1, n)
    def _(r):
        p = lax.rem(me + r, n)
        dt_chunk(p, me).wait_send()
        for unit in range(UNITS):
            chunk(unit, p, me).wait_send()

    for s in range(len(FACTORS)):
        sent_pair(halo_up(s), halo_down(s))
    sent_pair(coef_up, coef_down)


def on_device(n, cells, adjoint, grad, jac, c2, c4, dt, freq, damp):
    nv, lay, ny, nz = adjoint.shape[1:]
    rows = lay * ny // n
    assert rows * n == lay * ny and ny % rows == 0 and lay >= 2
    f32 = jnp.float32
    anywhere = pl.BlockSpec(memory_space=pl.ANY)
    sections = len(FACTORS)
    dma = pltpu.SemaphoreType.DMA
    tall = ny + 2 * PAD
    result = pl.pallas_call(
        functools.partial(kernel, n, cells),
        out_shape=jax.ShapeDtypeStruct(adjoint.shape[1:], f32),
        in_specs=[anywhere] * 8,
        out_specs=pl.BlockSpec(memory_space=pltpu.VMEM),
        scratch_shapes=[
            pltpu.VMEM((sections, nv, lay + 4, tall, nz), f32),
            pltpu.VMEM(jac.shape[1:], f32),
            pltpu.VMEM((2, lay + 4, ny, nz), f32),
            pltpu.VMEM((2, lay, tall, nz), f32),
            pltpu.VMEM((2, lay, ny, nz), f32),
            pltpu.VMEM((13, lay, ny, nz), f32),
            pltpu.VMEM((lay, ny, nz), f32),
            pltpu.VMEM((nv, lay, ny, nz), f32),
            pltpu.VMEM((nv, lay, ny, nz), f32),
            pltpu.VMEM((UNITS, n, nv * rows, nz), f32),
            pltpu.VMEM((UNITS, n, nv * rows, nz), f32),
            pltpu.VMEM((n, nv * rows, nz), f32),
            pltpu.VMEM((n, rows, nz), f32),
            pltpu.VMEM((n, rows, nz), f32),
            pltpu.SMEM((2 * n,), f32),
            pltpu.SMEM((1,), f32),
            pltpu.SMEM((1,), f32),
            dma((12,)),
            dma((UNITS, n)),
            dma((UNITS, n)),
            dma((n,)),
            dma((n,)),
            dma((sections, 2)),
            dma((sections, 2)),
            dma((2,)),
            dma((2,)),
        ],
        compiler_params=pltpu.CompilerParams(collective_id=0, has_side_effects=True),
    )(adjoint[0], grad[0], jac[0], c2[0], c4[0], dt[0], freq, damp)
    return result[None]


def solution(mesh):
    placed = (
        P("inst", None, "cells", None, None),
        P("inst", None, "cells", None, None),
        P("inst", None, None, None, "cells", None, None),
        P("inst", None, "cells", None, None),
        P("inst", None, "cells", None, None),
        P("inst", "cells", None, None),
        P(),
        P(),
    )
    return jax.shard_map(
        functools.partial(on_device, mesh.shape["inst"], mesh.shape["cells"]),
        mesh=mesh,
        in_specs=placed,
        out_specs=P("inst", None, "cells", None, None),
        check_vma=False,
    )
```

profile of v0, /device:TPU:0, one launch (start us, length us, event | category | flops | bytes accessed | tf_op | source)
XLA Modules:
  0.0 61.6 jit_solution(12802876579286380860)
XLA Ops:
  1.3 58.7 %shard_map.82 = f32[5,4,16,128]{3,2,1,0:T(8,128)} custom-call(f32[5,4,16,128]{3,2,1,0:T(8,128)} %bitcast.9, f32[5,4,16,128]{3,2,1,0:T(8,128)} %bitcast.10, f32[3,5,5,4,16,128]{5,4,3,2,1,0:T(8,128)} %bitcast.7, f32[3,4,16,128]{3,2,1,0:T(8,128)} %bitcast.11, f32[3,4,16,128]{3,2,1,0:T(8,128)} %bitcast.12, f32[4,16,128]{2,1,0:T(8,128)} %bitcast.13, ...), custom_call_target="tpu_custom_call" | custom-call | tf_op jit(solution)/shard_map/pallas_call | solution.py:429
  60.0 1.6 %copy.12 = f32[1,5,4,16,128]{4,3,2,1,0:T(8,128)} copy(f32[1,5,4,16,128]{4,3,2,1,0:T(8,128)} %bitcast.8) | data formatting | bytes 327680
where the time goes:
time: 61.8 us; the launch traced here: 61.6 us
  Pallas kernels  58.7 us (95%)
  local copies, waits for them, and re-layouts  1.59 us (3%)
  between operations  1.3 us (2%)
    pallas_call x1, Pallas kernels, on_device(): pl.pallas_call(functools.partial(kernel, n, cells), out_shape=jax.ShapeDt...  58.7 us
    unnamed x1, local copies, waits for them, and re-layouts  1.59 us

commit v1 on v0

v1 whole, which is shorter than its diff:
```python
import functools
import math

import jax
import jax.numpy as jnp
from jax import lax
from jax.experimental import pallas as pl
from jax.experimental.pallas import tpu as pltpu
from jax.sharding import PartitionSpec as P

FACTORS = (0.25, 1.0 / 6.0, 0.375, 0.5, 1.0)
SECTIONS = len(FACTORS)
PAD = 8
TILE = 8
MESH = pl.DeviceIdType.MESH


def coupling_tables(count):
    slope, curve = [0.0], [count * count / 12.0 + 1.0 / 6.0]
    for m in range(1, count):
        parity = 1.0 if m % 2 == 0 else -1.0
        angle = math.pi * m / count
        slope.append(0.5 * parity * math.cos(angle) / math.sin(angle))
        curve.append(0.5 * parity / math.sin(angle) ** 2)
    return slope, curve


def kernel(
    n, cells, adj, grad, jac, c2, c4, dt, freq_in, damp_in, out,
    vp, jv, cx, cy, cz, kk, gv, uh, mh, tb, mt, hb, kv, freq, damp,
    loc_sem, ss, trs, mrs, hss, hrs, chs, chr_,
):
    nv, lay, ny, nz = adj.shape
    rows = lay * ny // n
    per = ny // rows
    pack = TILE // rows
    groups = n // pack
    me = lax.axis_index("inst")
    cell = lax.axis_index("cells")
    has_lo = cell > 0
    has_hi = cell < cells - 1
    lo = has_lo.astype(jnp.int32)
    hi = has_hi.astype(jnp.int32)
    both = lo * hi
    back = lo * (1 - both)
    mid = slice(PAD, PAD + ny)

    def mirror(value, step, count):
        if count & (count - 1):
            return lax.rem(value + 1 + step, count)
        flip, total, bit = count - 1 - step, 0, 1
        while bit < count:
            total = total + lax.rem(value // bit + flip // bit, 2) * bit
            bit *= 2
        return total

    barrier = pltpu.get_barrier_semaphore()

    @pl.loop(0, n - 1)
    def _(i):
        pl.semaphore_signal(barrier, inc=1, device_id={"inst": mirror(me, i, n)}, device_id_type=MESH)

    @pl.when(has_lo)
    def _():
        pl.semaphore_signal(barrier, inc=1, device_id={"cells": cell - 1}, device_id_type=MESH)

    @pl.when(has_hi)
    def _():
        pl.semaphore_signal(barrier, inc=1, device_id={"cells": cell + 1}, device_id_type=MESH)

    local = [
        (adj, vp.at[0, :, 2 : 2 + lay, mid, :]),
        (dt, uh.at[0, nv]),
        (c2.at[0], cx.at[0, 2 : 2 + lay]),
        (c4.at[0], cx.at[1, 2 : 2 + lay]),
        (c2.at[1], cy.at[0, :, mid, :]),
        (c4.at[1], cy.at[1, :, mid, :]),
        (c2.at[2], cz.at[0]),
        (c4.at[2], cz.at[1]),
        (grad, gv),
        (jac, jv),
        (freq_in, freq),
        (damp_in, damp),
    ]
    local = [pltpu.make_async_copy(s, d, loc_sem.at[i]) for i, (s, d) in enumerate(local)]
    for c in local:
        c.start()
    dtv = uh.at[0, nv]

    def wait_bytes(ref, sem):
        pltpu.make_async_copy(ref, ref, sem).wait()

    def width(unit):
        return nv + 1 if unit == 1 else nv

    def spot(p):
        return lax.rem(p, lay), pl.multiple_of((p // lay) * rows, rows)

    def owner_rows(p):
        return pl.ds(pl.multiple_of(p * rows, rows), rows)

    def outbound(unit, p):
        x, y = spot(p)
        if unit == 0:
            src = vp.at[0, :, 2 + x, pl.ds(PAD + y, rows), :]
        else:
            src = uh.at[unit - 1, 0 : width(unit), x, pl.ds(y, rows), :]
        return src, tb.at[unit, 0 : width(unit), owner_rows(me), :]

    def send_out(unit, p):
        src, dst = outbound(unit, p)

        @pl.when(p != me)
        def _():
            pltpu.make_async_remote_copy(
                src_ref=src, dst_ref=dst, send_sem=ss.at[unit], recv_sem=trs.at[unit],
                device_id={"inst": p}, device_id_type=MESH,
            ).start()

        @pl.when(p == me)
        def _():
            pltpu.make_async_copy(src, dst, trs.at[unit]).start()

    def send_home(s):
        x, y = spot(me)
        dst = mh.at[s, :, x, pl.ds(y, rows), :]

        @pl.loop(0, n - 1)
        def _(i):
            p = mirror(me, i, n)
            pltpu.make_async_remote_copy(
                src_ref=mt.at[s, :, owner_rows(p), :], dst_ref=dst,
                send_sem=ss.at[SECTIONS + s], recv_sem=mrs.at[s, x],
                device_id={"inst": p}, device_id_type=MESH,
            ).start()

        pltpu.make_async_copy(mt.at[s, :, owner_rows(me), :], dst, mrs.at[s, x]).start()

    def halo_up(s):
        return pltpu.make_async_remote_copy(
            src_ref=vp.at[s, :, lay : lay + 2, mid, :], dst_ref=hb.at[s, 0],
            send_sem=hss.at[s, 0], recv_sem=hrs.at[s, 0],
            device_id={"cells": cell + 1}, device_id_type=MESH,
        )

    def halo_down(s):
        return pltpu.make_async_remote_copy(
            src_ref=vp.at[s, :, 2:4, mid, :], dst_ref=hb.at[s, 1],
            send_sem=hss.at[s, 1], recv_sem=hrs.at[s, 1],
            device_id={"cells": cell - 1}, device_id_type=MESH,
        )

    coef_up = pltpu.make_async_remote_copy(
        src_ref=cx.at[:, lay : lay + 2], dst_ref=cx.at[:, 0:2],
        send_sem=chs.at[0], recv_sem=chr_.at[0],
        device_id={"cells": cell + 1}, device_id_type=MESH,
    )
    coef_down = pltpu.make_async_remote_copy(
        src_ref=cx.at[:, 2:4], dst_ref=cx.at[:, 2 + lay : 4 + lay],
        send_sem=chs.at[1], recv_sem=chr_.at[1],
        device_id={"cells": cell - 1}, device_id_type=MESH,
    )

    def start_pair(up, down):
        @pl.when(has_hi)
        def _():
            up.start()

        @pl.when(has_lo)
        def _():
            down.start()

    def land_pair(up, down):
        @pl.when(has_lo)
        def _():
            up.wait_recv()

        @pl.when(has_hi)
        def _():
            down.wait_recv()

    def sent_pair(up, down):
        @pl.when(has_hi)
        def _():
            up.wait_send()

        @pl.when(has_lo)
        def _():
            down.wait_send()

    lanes = lax.broadcasted_iota(jnp.int32, (ny, nz), 1)
    keep_lo = jnp.where(lanes >= 1, 1.0, 0.0)
    keep_hi = jnp.where(lanes < nz - 1, 1.0, 0.0)

    def stencil_plane():
        @pl.loop(0, lay)
        def _(x):
            up4 = cy[1, x, PAD + 1 : PAD + 1 + ny, :]
            here3 = 3.0 * cy[1, x, mid, :] + cy[0, x, mid, :]
            low = slice(PAD - 1, PAD - 1 + ny)
            below3 = 3.0 * cy[1, x, low, :] + cy[0, x, low, :]
            below4 = cy[1, x, PAD - 2 : PAD - 2 + ny, :]
            kk[4, x] = below4
            kk[5, x] = -(below3 + below4)
            kk[6, x] = -(up4 + here3)
            kk[7, x] = up4
            centre = here3 + below3
            here4 = cz[1, x]
            here3 = 3.0 * here4 + cz[0, x]
            up4 = jnp.where(lanes < nz - 1, pltpu.roll(here4, nz - 1, 1), 0.0)
            below3 = jnp.where(lanes >= 1, pltpu.roll(here3, 1, 1), 0.0)
            below4 = jnp.where(lanes >= 2, pltpu.roll(here4, 2, 1), 0.0)
            kk[8, x] = below4
            kk[9, x] = jnp.where(lanes >= 1, -(below3 + below4), 0.0)
            kk[10, x] = jnp.where(lanes < nz - 1, -(up4 + here3), 0.0)
            kk[11, x] = jnp.where(lanes < nz - 2, up4, 0.0)
            kk[12, x] = centre + here3 + below3

    def stencil_layers():
        @pl.loop(0, lay)
        def _(x):
            up4 = cx[1, x + 3]
            here3 = 3.0 * cx[1, x + 2] + cx[0, x + 2]
            below3 = 3.0 * cx[1, x + 1] + cx[0, x + 1]
            below4 = cx[1, x]
            kk[0, x] = below4
            kk[1, x] = -(below3 + below4)
            kk[2, x] = -(up4 + here3)
            kk[3, x] = up4
            kk[12, x] += here3 + below3

    def send_layer(s, x):
        for i in range(per):
            send_out(s + 1, mirror(me // lay, i, per) * lay + x)

    def spatial(s, sending):
        factor = FACTORS[s]
        first, last = 2 * lo, lay - 2 * hi

        @pl.loop(0, lay)
        def _(i):
            x = back * (lay - 1 - i) + (1 - back) * i
            sums, central = [], [[], [], []]
            for b in range(nv):
                v0 = vp[s, b, x + 2, mid, :]
                total = kk[12, x] * v0 + gv[b, x]
                m2, m1 = vp[s, b, x, mid, :], vp[s, b, x + 1, mid, :]
                p1, p2 = vp[s, b, x + 3, mid, :], vp[s, b, x + 4, mid, :]
                total += kk[0, x] * m2 + kk[1, x] * m1 + kk[2, x] * p1 + kk[3, x] * p2
                central[0].append(m1 - p1)
                m2, m1, p1, p2 = (
                    vp[s, b, x + 2, PAD + o : PAD + o + ny, :] for o in (-2, -1, 1, 2)
                )
                total += kk[4, x] * m2 + kk[5, x] * m1 + kk[6, x] * p1 + kk[7, x] * p2
                central[1].append(m1 - p1)
                m2, m1, p1, p2 = (pltpu.roll(v0, o, 1) for o in (2, 1, nz - 1, nz - 2))
                total += kk[8, x] * m2 + kk[9, x] * m1 + kk[10, x] * p1 + kk[11, x] * p2
                central[2].append(keep_lo * m1 - keep_hi * p1)
                sums.append(total)
            step = factor * dtv[x]
            for b in range(nv):
                flux = jv[0, 0, b, x] * central[0][0]
                for d in range(3):
                    for a in range(nv):
                        if d or a:
                            flux += jv[d, a, b, x] * central[d][a]
                uh[s, b, x] = vp[0, b, x + 2, mid, :] - step * (sums[b] + 0.5 * flux)

            if sending:
                @pl.when(jnp.logical_and(x >= first, x < last))
                def _():
                    send_layer(s, x)

        def edge(x, side, near, far, k_near, k_far, sign):
            step = factor * dtv[x]
            for b in range(nv):
                flux = jv[0, 0, b, x] * hb[s, side, 0, near]
                for a in range(1, nv):
                    flux += jv[0, a, b, x] * hb[s, side, a, near]
                total = kk[k_near, x] * hb[s, side, b, near] + kk[k_far, x] * hb[s, side, b, far]
                uh[s, b, x] -= step * (total + sign * flux)

        def rim(x, side, near, k_far):
            step = factor * dtv[x]
            for b in range(nv):
                uh[s, b, x] -= step * (kk[k_far, x] * hb[s, side, b, near])

        @pl.when(has_lo)
        def _():
            halo_up(s).wait_recv()
            edge(0, 0, 1, 0, 1, 0, 0.5)
            rim(1, 0, 1, 0)

        @pl.when(has_hi)
        def _():
            halo_down(s).wait_recv()
            edge(lay - 1, 1, 0, 1, 2, 3, -0.5)
            rim(lay - 2, 1, 0, 3)

        if sending:
            @pl.loop(0, lay)
            def _(x):
                @pl.when(jnp.logical_or(x < first, x >= last))
                def _():
                    send_layer(s, x)

    def home_step(s):
        factor = FACTORS[s - 1]
        ready = 2 * (1 - both) + lay * both

        @pl.loop(0, lay)
        def _(i):
            x = back * i + (1 - back) * (lay - 1 - i)
            wait_bytes(mh.at[s - 1, :, x], mrs.at[s - 1, x])
            step = factor * dtv[x]
            for b in range(nv):
                vp[s, b, 2 + x, mid, :] = uh[s - 1, b, x] - step * mh[s - 1, b, x]

            @pl.when(i == ready - 1)
            def _():
                start_pair(halo_up(s), halo_down(s))

    def mix(s, value):
        @pl.loop(0, nv)
        def _(b):
            weights = [kv[i] for i in range(n)]
            turned = []
            for j in range(groups):
                v = value(b, slice(j * TILE, (j + 1) * TILE))
                turned.append([v] + [pltpu.roll(v, TILE - r * rows, 0) for r in range(1, pack)])
            for k in range(groups):
                total = None
                for j in range(groups):
                    for r in range(pack):
                        term = weights[(j - k) % groups * pack + r] * turned[j][r]
                        total = term if total is None else total + term
                mt[s, b, k * TILE : (k + 1) * TILE, :] = total

        send_home(s)

    def owner_start():
        wait_bytes(tb.at[0, 0:nv], trs.at[0])
        mix(0, lambda b, r: tb[0, b, r, :])

    def owner_step(s):
        wait_bytes(tb.at[s, 0 : width(s)], trs.at[s])
        factor = FACTORS[s - 1]
        mix(s, lambda b, r: tb[s, b, r, :] - factor * (tb[1, nv, r, :] * mt[s - 1, b, r, :]))

    slope, curve = coupling_tables(n)
    part = lax.broadcasted_iota(jnp.int32, (TILE, nz), 0) // rows
    local[10].wait()
    local[11].wait()
    for j in range(groups):
        for r in range(pack):
            rise = jnp.zeros((TILE, nz), jnp.float32)
            bend = jnp.zeros((TILE, nz), jnp.float32)
            for h in range(pack):
                m = (j * pack + (h + r) % pack - h) % n
                rise = jnp.where(part == h, slope[m], rise)
                bend = jnp.where(part == h, curve[m], bend)
            kv[j * pack + r] = freq[0] * rise + damp[0] * bend
    for s in range(SECTIONS):
        vp[s, :, 2 : 2 + lay, 0:PAD, :] = jnp.zeros((nv, lay, PAD, nz), jnp.float32)
        vp[s, :, 2 : 2 + lay, PAD + ny :, :] = jnp.zeros((nv, lay, PAD, nz), jnp.float32)
        vp[s, :, 0:2, mid, :] = jnp.zeros((nv, 2, ny, nz), jnp.float32)
        vp[s, :, 2 + lay :, mid, :] = jnp.zeros((nv, 2, ny, nz), jnp.float32)
    cy[:, :, 0:PAD, :] = jnp.zeros((2, lay, PAD, nz), jnp.float32)
    cy[:, :, PAD + ny :, :] = jnp.zeros((2, lay, PAD, nz), jnp.float32)

    @pl.when(jnp.logical_not(has_lo))
    def _():
        cx[:, 0:2] = jnp.zeros((2, 2, ny, nz), jnp.float32)

    @pl.when(jnp.logical_not(has_hi))
    def _():
        cx[:, 2 + lay :] = jnp.zeros((2, 2, ny, nz), jnp.float32)

    local[0].wait()
    local[2].wait()
    local[3].wait()
    pl.semaphore_wait(barrier, n - 1 + lo + hi)

    @pl.loop(0, n)
    def _(i):
        send_out(0, mirror(me, i, n))

    start_pair(coef_up, coef_down)
    start_pair(halo_up(0), halo_down(0))
    for c in [local[1]] + local[4:10]:
        c.wait()
    stencil_plane()
    land_pair(coef_up, coef_down)
    stencil_layers()
    spatial(0, True)
    owner_start()
    owner_step(1)
    home_step(1)
    spatial(1, True)
    home_step(2)
    spatial(2, True)
    owner_step(2)
    owner_step(3)
    home_step(3)
    spatial(3, True)
    home_step(4)
    spatial(4, False)
    owner_step(4)

    @pl.loop(0, lay)
    def _(x):
        wait_bytes(mh.at[4, :, x], mrs.at[4, x])
        step = FACTORS[4] * dtv[x]
        for b in range(nv):
            out[b, x] = uh[4, b, x] - step * mh[4, b, x]

    for unit in range(SECTIONS):
        wait_bytes(tb.at[unit, 0 : width(unit), 0 : (n - 1) * rows, :], ss.at[unit])
        wait_bytes(mt.at[unit, :, 0 : (n - 1) * rows, :], ss.at[SECTIONS + unit])
    for s in range(SECTIONS):
        sent_pair(halo_up(s), halo_down(s))
    sent_pair(coef_up, coef_down)


def on_device(n, cells, adjoint, grad, jac, c2, c4, dt, freq, damp):
    nv, lay, ny, nz = adjoint.shape[1:]
    rows = lay * ny // n
    assert rows * n == lay * ny and ny % rows == 0 and lay >= 2
    assert TILE % rows == 0 and (n * rows) % TILE == 0
    f32 = jnp.float32
    anywhere = pl.BlockSpec(memory_space=pl.ANY)
    dma = pltpu.SemaphoreType.DMA
    tall = ny + 2 * PAD
    result = pl.pallas_call(
        functools.partial(kernel, n, cells),
        out_shape=jax.ShapeDtypeStruct(adjoint.shape[1:], f32),
        in_specs=[anywhere] * 8,
        out_specs=pl.BlockSpec(memory_space=pltpu.VMEM),
        scratch_shapes=[
            pltpu.VMEM((SECTIONS, nv, lay + 4, tall, nz), f32),
            pltpu.VMEM(jac.shape[1:], f32),
            pltpu.VMEM((2, lay + 4, ny, nz), f32),
            pltpu.VMEM((2, lay, tall, nz), f32),
            pltpu.VMEM((2, lay, ny, nz), f32),
            pltpu.VMEM((13, lay, ny, nz), f32),
            pltpu.VMEM((nv, lay, ny, nz), f32),
            pltpu.VMEM((SECTIONS, nv + 1, lay, ny, nz), f32),
            pltpu.VMEM((SECTIONS, nv, lay, ny, nz), f32),
            pltpu.VMEM((SECTIONS, nv + 1, n * rows, nz), f32),
            pltpu.VMEM((SECTIONS, nv, n * rows, nz), f32),
            pltpu.VMEM((SECTIONS, 2, nv, 2, ny, nz), f32),
            pltpu.VMEM((n, TILE, nz), f32),
            pltpu.SMEM((1,), f32),
            pltpu.SMEM((1,), f32),
            dma((12,)),
            dma((2 * SECTIONS,)),
            dma((SECTIONS,)),
            dma((SECTIONS, lay)),
            dma((SECTIONS, 2)),
            dma((SECTIONS, 2)),
            dma((2,)),
            dma((2,)),
        ],
        compiler_params=pltpu.CompilerParams(collective_id=0, has_side_effects=True),
    )(adjoint[0], grad[0], jac[0], c2[0], c4[0], dt[0], freq, damp)
    return result[None]


def solution(mesh):
    placed = (
        P("inst", None, "cells", None, None),
        P("inst", None, "cells", None, None),
        P("inst", None, None, None, "cells", None, None),
        P("inst", None, "cells", None, None),
        P("inst", None, "cells", None, None),
        P("inst", "cells", None, None),
        P(),
        P(),
    )
    return jax.shard_map(
        functools.partial(on_device, mesh.shape["inst"], mesh.shape["cells"]),
        mesh=mesh,
        in_specs=placed,
        out_specs=P("inst", None, "cells", None, None),
        check_vma=False,
    )
```

time: 61.8 us -> 52.2 us (0.84)
  Pallas kernels: 58.7 us -> 49.1 us
    pallas_call x1, Pallas kernels: 58.7 us -> 49.1 us  [on_device(): pl.pallas_call(functools.partial(kernel, n, cells), out_shape=jax.ShapeDt...]
where the time goes in v1:
time: 52.2 us; the launch traced here: 52 us
  Pallas kernels  49.1 us (94%)
  local copies, waits for them, and re-layouts  1.59 us (3%)
  between operations  1.3 us (2%)
    pallas_call x1, Pallas kernels, on_device(): pl.pallas_call(functools.partial(kernel, n, cells), out_shape=jax.ShapeDt...  49.1 us
    unnamed x1, local copies, waits for them, and re-layouts  1.59 us

profile of v1, /device:TPU:0, one launch (start us, length us, event | category | flops | bytes accessed | tf_op | source)
XLA Modules:
  0.0 52.0 jit_solution(9573826597265503324)
XLA Ops:
  1.3 49.1 %shard_map.82 = f32[5,4,16,128]{3,2,1,0:T(8,128)} custom-call(f32[5,4,16,128]{3,2,1,0:T(8,128)} %bitcast.9, f32[5,4,16,128]{3,2,1,0:T(8,128)} %bitcast.10, f32[3,5,5,4,16,128]{5,4,3,2,1,0:T(8,128)} %bitcast.7, f32[3,4,16,128]{3,2,1,0:T(8,128)} %bitcast.11, f32[3,4,16,128]{3,2,1,0:T(8,128)} %bitcast.12, f32[4,16,128]{2,1,0:T(8,128)} %bitcast.13, ...), custom_call_target="tpu_custom_call" | custom-call | tf_op jit(solution)/shard_map/pallas_call | solution.py:434
  50.5 1.6 %copy.12 = f32[1,5,4,16,128]{4,3,2,1,0:T(8,128)} copy(f32[1,5,4,16,128]{4,3,2,1,0:T(8,128)} %bitcast.8) | data formatting | bytes 327680

commit v2 on v1

--- a/solution.py
+++ b/solution.py
@@ -45,20 +45,36 @@
     back = lo * (1 - both)
     mid = slice(PAD, PAD + ny)
 
-    def mirror(value, step, count):
+    def mirrors(value, count):
         if count & (count - 1):
-            return lax.rem(value + 1 + step, count)
-        flip, total, bit = count - 1 - step, 0, 1
+            return [lax.rem(value + i, count) for i in range(1, count)]
+        moves, bit = [], 1
         while bit < count:
-            total = total + lax.rem(value // bit + flip // bit, 2) * bit
+            moves.append((bit, bit - 2 * bit * lax.rem(lax.div(value, bit), 2)))
             bit *= 2
-        return total
+        found = []
+        for flip in range(count - 1, 0, -1):
+            other = value
+            for bit, move in moves:
+                if flip & bit:
+                    other = other + move
+            found.append(other)
+        return found
+
+    def spot(p):
+        q = lax.div(p, lay)
+        return lax.rem(p + q, lay), pl.multiple_of(q * rows, rows)
+
+    others = mirrors(me, n)
+    spots = [spot(p) for p in others]
+    home_x, home_y = spot(me)
+    own_q = lax.div(me, lay)
+    turns = mirrors(own_q, per) + [own_q]
 
     barrier = pltpu.get_barrier_semaphore()
 
-    @pl.loop(0, n - 1)
-    def _(i):
-        pl.semaphore_signal(barrier, inc=1, device_id={"inst": mirror(me, i, n)}, device_id_type=MESH)
+    for p in others:
+        pl.semaphore_signal(barrier, inc=1, device_id={"inst": p}, device_id_type=MESH)
 
     @pl.when(has_lo)
     def _():
@@ -93,48 +109,36 @@
     def width(unit):
         return nv + 1 if unit == 1 else nv
 
-    def spot(p):
-        return lax.rem(p, lay), pl.multiple_of((p // lay) * rows, rows)
-
     def owner_rows(p):
         return pl.ds(pl.multiple_of(p * rows, rows), rows)
 
-    def outbound(unit, p):
-        x, y = spot(p)
+    def chunk_at(unit, x, y):
         if unit == 0:
-            src = vp.at[0, :, 2 + x, pl.ds(PAD + y, rows), :]
-        else:
-            src = uh.at[unit - 1, 0 : width(unit), x, pl.ds(y, rows), :]
-        return src, tb.at[unit, 0 : width(unit), owner_rows(me), :]
-
-    def send_out(unit, p):
-        src, dst = outbound(unit, p)
-
-        @pl.when(p != me)
-        def _():
+            return vp.at[0, :, 2 + x, pl.ds(pl.multiple_of(PAD + y, rows), rows), :]
+        return uh.at[unit - 1, 0 : width(unit), x, pl.ds(y, rows), :]
+
+    def send_out(unit, p, x, y):
+        pltpu.make_async_remote_copy(
+            src_ref=chunk_at(unit, x, y), dst_ref=tb.at[unit, 0 : width(unit), owner_rows(me), :],
+            send_sem=ss.at[unit], recv_sem=trs.at[unit],
+            device_id={"inst": p}, device_id_type=MESH,
+        ).start()
+
+    def keep_out(unit):
+        pltpu.make_async_copy(
+            chunk_at(unit, home_x, home_y), tb.at[unit, 0 : width(unit), owner_rows(me), :],
+            trs.at[unit],
+        ).start()
+
+    def send_home(s):
+        dst = mh.at[s, :, home_x, pl.ds(home_y, rows), :]
+        for p in others:
             pltpu.make_async_remote_copy(
-                src_ref=src, dst_ref=dst, send_sem=ss.at[unit], recv_sem=trs.at[unit],
+                src_ref=mt.at[s, :, owner_rows(p), :], dst_ref=dst,
+                send_sem=ss.at[SECTIONS + s], recv_sem=mrs.at[s, home_x],
                 device_id={"inst": p}, device_id_type=MESH,
             ).start()
-
-        @pl.when(p == me)
-        def _():
-            pltpu.make_async_copy(src, dst, trs.at[unit]).start()
-
-    def send_home(s):
-        x, y = spot(me)
-        dst = mh.at[s, :, x, pl.ds(y, rows), :]
-
-        @pl.loop(0, n - 1)
-        def _(i):
-            p = mirror(me, i, n)
-            pltpu.make_async_remote_copy(
-                src_ref=mt.at[s, :, owner_rows(p), :], dst_ref=dst,
-                send_sem=ss.at[SECTIONS + s], recv_sem=mrs.at[s, x],
-                device_id={"inst": p}, device_id_type=MESH,
-            ).start()
-
-        pltpu.make_async_copy(mt.at[s, :, owner_rows(me), :], dst, mrs.at[s, x]).start()
+        pltpu.make_async_copy(mt.at[s, :, owner_rows(me), :], dst, mrs.at[s, home_x]).start()
 
     def halo_up(s):
         return pltpu.make_async_remote_copy(
@@ -230,8 +234,19 @@
             kk[12, x] += here3 + below3
 
     def send_layer(s, x):
-        for i in range(per):
-            send_out(s + 1, mirror(me // lay, i, per) * lay + x)
+        for i, q in enumerate(turns):
+            p = q * lay + lax.rem(x + (lay * per - q), lay)
+            y = pl.multiple_of(q * rows, rows)
+            if i < per - 1:
+                send_out(s + 1, p, x, y)
+            else:
+                @pl.when(x != home_x)
+                def _():
+                    send_out(s + 1, p, x, y)
+
+                @pl.when(x == home_x)
+                def _():
+                    keep_out(s + 1)
 
     def spatial(s, sending):
         factor = FACTORS[s]
@@ -381,10 +396,9 @@
     local[3].wait()
     pl.semaphore_wait(barrier, n - 1 + lo + hi)
 
-    @pl.loop(0, n)
-    def _(i):
-        send_out(0, mirror(me, i, n))
-
+    for p, (x, y) in zip(others, spots):
+        send_out(0, p, x, y)
+    keep_out(0)
     start_pair(coef_up, coef_down)
     start_pair(halo_up(0), halo_down(0))
     for c in [local[1]] + local[4:10]:

time: 52.2 us -> 51 us (0.977)
  Pallas kernels: 49.1 us -> 48 us
    pallas_call x1, Pallas kernels: 49.1 us -> 48 us  [on_device(): pl.pallas_call(functools.partial(kernel, n, cells), out_shape=jax.ShapeDt...]
where the time goes in v2:
time: 51 us; the launch traced here: 50.9 us
  Pallas kernels  48 us (94%)
  local copies, waits for them, and re-layouts  1.59 us (3%)
  between operations  1.3 us (3%)
    pallas_call x1, Pallas kernels, on_device(): pl.pallas_call(functools.partial(kernel, n, cells), out_shape=jax.ShapeDt...  48 us
    unnamed x1, local copies, waits for them, and re-layouts  1.59 us

profile of v2, /device:TPU:0, one launch (start us, length us, event | category | flops | bytes accessed | tf_op | source)
XLA Modules:
  0.0 50.9 jit_solution(11030601834445953120)
XLA Ops:
  1.3 48.0 %shard_map.82 = f32[5,4,16,128]{3,2,1,0:T(8,128)} custom-call(f32[5,4,16,128]{3,2,1,0:T(8,128)} %bitcast.9, f32[5,4,16,128]{3,2,1,0:T(8,128)} %bitcast.10, f32[3,5,5,4,16,128]{5,4,3,2,1,0:T(8,128)} %bitcast.7, f32[3,4,16,128]{3,2,1,0:T(8,128)} %bitcast.11, f32[3,4,16,128]{3,2,1,0:T(8,128)} %bitcast.12, f32[4,16,128]{2,1,0:T(8,128)} %bitcast.13, ...), custom_call_target="tpu_custom_call" | custom-call | tf_op jit(solution)/shard_map/pallas_call | solution.py:448
  49.3 1.6 %copy.12 = f32[1,5,4,16,128]{4,3,2,1,0:T(8,128)} copy(f32[1,5,4,16,128]{4,3,2,1,0:T(8,128)} %bitcast.8) | data formatting | bytes 327680

commit v3 on v2

--- a/solution.py
+++ b/solution.py
@@ -447,7 +447,7 @@
     tall = ny + 2 * PAD
     result = pl.pallas_call(
         functools.partial(kernel, n, cells),
-        out_shape=jax.ShapeDtypeStruct(adjoint.shape[1:], f32),
+        out_shape=pltpu.VMEM(adjoint.shape[1:], f32),
         in_specs=[anywhere] * 8,
         out_specs=pl.BlockSpec(memory_space=pltpu.VMEM),
         scratch_shapes=[

time: 51 us -> 49.4 us (0.969)
  local copies, waits for them, and re-layouts: 1.59 us -> 0.67 us
  Pallas kernels: 48 us -> 47.3 us
    unnamed x1, local copies, waits for them, and re-layouts: 1.59 us -> 0.67 us
    pallas_call x1, Pallas kernels: 48 us -> 47.3 us  [on_device(): pl.pallas_call(functools.partial(kernel, n, cells), out_shape=pltpu.VMEM(...]
where the time goes in v3:
time: 49.4 us; the launch traced here: 49.3 us
  Pallas kernels  47.3 us (96%)
  between operations  1.3 us (3%)
  local copies, waits for them, and re-layouts  0.67 us (1%)
    pallas_call x1, Pallas kernels, on_device(): pl.pallas_call(functools.partial(kernel, n, cells), out_shape=pltpu.VMEM(...  47.3 us

profile of v3, /device:TPU:0, one launch (start us, length us, event | category | flops | bytes accessed | tf_op | source)
XLA Modules:
  0.0 49.3 jit_solution(14574293387173907854)
XLA Ops:
  1.3 47.3 %shard_map.82 = f32[5,4,16,128]{3,2,1,0:T(8,128)S(1)} custom-call(f32[5,4,16,128]{3,2,1,0:T(8,128)} %bitcast.9, f32[5,4,16,128]{3,2,1,0:T(8,128)} %bitcast.10, f32[3,5,5,4,16,128]{5,4,3,2,1,0:T(8,128)} %bitcast.8, f32[3,4,16,128]{3,2,1,0:T(8,128)} %bitcast.11, f32[3,4,16,128]{3,2,1,0:T(8,128)} %bitcast.12, f32[4,16,128]{2,1,0:T(8,128)} %bitcast.13, ...), custom_call_target="tpu_custom_call" | custom-call | tf_op jit(solution)/shard_map/pallas_call | solution.py:448
  48.6 0.7 %copy.10 = f32[1,5,4,16,128]{4,3,2,1,0:T(8,128)} copy(f32[1,5,4,16,128]{4,3,2,1,0:T(8,128)S(1)} %bitcast.7) | data formatting | bytes 327680

commit v4 on v3

--- a/solution.py
+++ b/solution.py
@@ -362,6 +362,11 @@
         factor = FACTORS[s - 1]
         mix(s, lambda b, r: tb[s, b, r, :] - factor * (tb[1, nv, r, :] * mt[s - 1, b, r, :]))
 
+    def send_all(s):
+        @pl.loop(0, lay)
+        def _(x):
+            send_layer(s, x)
+
     slope, curve = coupling_tables(n)
     part = lax.broadcasted_iota(jnp.int32, (TILE, nz), 0) // rows
     local[10].wait()
@@ -406,20 +411,21 @@
     stencil_plane()
     land_pair(coef_up, coef_down)
     stencil_layers()
-    spatial(0, True)
+    spatial(0, False)
     owner_start()
-    owner_step(1)
+    send_all(0)
     home_step(1)
     spatial(1, True)
+    owner_step(1)
+    owner_step(2)
     home_step(2)
     spatial(2, True)
-    owner_step(2)
-    owner_step(3)
     home_step(3)
     spatial(3, True)
+    owner_step(3)
+    owner_step(4)
     home_step(4)
     spatial(4, False)
-    owner_step(4)
 
     @pl.loop(0, lay)
     def _(x):

time: 49.4 us -> 48.8 us (0.988)
  Pallas kernels: 47.3 us -> 46.7 us
    pallas_call x1, Pallas kernels: 47.3 us -> 46.7 us  [on_device(): pl.pallas_call(functools.partial(kernel, n, cells), out_shape=pltpu.VMEM(...]
where the time goes in v4:
time: 48.8 us; the launch traced here: 48.6 us
  Pallas kernels  46.7 us (96%)
  between operations  1.3 us (3%)
  local copies, waits for them, and re-layouts  0.67 us (1%)
    pallas_call x1, Pallas kernels, on_device(): pl.pallas_call(functools.partial(kernel, n, cells), out_shape=pltpu.VMEM(...  46.7 us

profile of v4, /device:TPU:0, one launch (start us, length us, event | category | flops | bytes accessed | tf_op | source)
XLA Modules:
  0.0 48.6 jit_solution(5844681504786000588)
XLA Ops:
  1.3 46.7 %shard_map.82 = f32[5,4,16,128]{3,2,1,0:T(8,128)S(1)} custom-call(f32[5,4,16,128]{3,2,1,0:T(8,128)} %bitcast.9, f32[5,4,16,128]{3,2,1,0:T(8,128)} %bitcast.10, f32[3,5,5,4,16,128]{5,4,3,2,1,0:T(8,128)} %bitcast.8, f32[3,4,16,128]{3,2,1,0:T(8,128)} %bitcast.11, f32[3,4,16,128]{3,2,1,0:T(8,128)} %bitcast.12, f32[4,16,128]{2,1,0:T(8,128)} %bitcast.13, ...), custom_call_target="tpu_custom_call" | custom-call | tf_op jit(solution)/shard_map/pallas_call | solution.py:454
  48.0 0.7 %copy.10 = f32[1,5,4,16,128]{4,3,2,1,0:T(8,128)} copy(f32[1,5,4,16,128]{4,3,2,1,0:T(8,128)S(1)} %bitcast.7) | data formatting | bytes 327680

commit v5 on v4

--- a/solution.py
+++ b/solution.py
@@ -106,28 +106,37 @@
     def wait_bytes(ref, sem):
         pltpu.make_async_copy(ref, ref, sem).wait()
 
-    def width(unit):
-        return nv + 1 if unit == 1 else nv
-
     def owner_rows(p):
         return pl.ds(pl.multiple_of(p * rows, rows), rows)
 
     def chunk_at(unit, x, y):
         if unit == 0:
             return vp.at[0, :, 2 + x, pl.ds(pl.multiple_of(PAD + y, rows), rows), :]
-        return uh.at[unit - 1, 0 : width(unit), x, pl.ds(y, rows), :]
+        return uh.at[unit - 1, 0:nv, x, pl.ds(y, rows), :]
 
     def send_out(unit, p, x, y):
         pltpu.make_async_remote_copy(
-            src_ref=chunk_at(unit, x, y), dst_ref=tb.at[unit, 0 : width(unit), owner_rows(me), :],
+            src_ref=chunk_at(unit, x, y), dst_ref=tb.at[unit, 0:nv, owner_rows(me), :],
             send_sem=ss.at[unit], recv_sem=trs.at[unit],
             device_id={"inst": p}, device_id_type=MESH,
         ).start()
 
     def keep_out(unit):
         pltpu.make_async_copy(
-            chunk_at(unit, home_x, home_y), tb.at[unit, 0 : width(unit), owner_rows(me), :],
+            chunk_at(unit, home_x, home_y), tb.at[unit, 0:nv, owner_rows(me), :],
             trs.at[unit],
+        ).start()
+
+    def send_steps():
+        dst = tb.at[1, nv, owner_rows(me), :]
+        for p, (x, y) in zip(others, spots):
+            pltpu.make_async_remote_copy(
+                src_ref=uh.at[0, nv, x, pl.ds(y, rows), :], dst_ref=dst,
+                send_sem=ss.at[2 * SECTIONS], recv_sem=trs.at[SECTIONS],
+                device_id={"inst": p}, device_id_type=MESH,
+            ).start()
+        pltpu.make_async_copy(
+            uh.at[0, nv, home_x, pl.ds(home_y, rows), :], dst, trs.at[SECTIONS]
         ).start()
 
     def send_home(s):
@@ -358,7 +367,9 @@
         mix(0, lambda b, r: tb[0, b, r, :])
 
     def owner_step(s):
-        wait_bytes(tb.at[s, 0 : width(s)], trs.at[s])
+        wait_bytes(tb.at[s, 0:nv], trs.at[s])
+        if s == 1:
+            wait_bytes(tb.at[1, nv], trs.at[SECTIONS])
         factor = FACTORS[s - 1]
         mix(s, lambda b, r: tb[s, b, r, :] - factor * (tb[1, nv, r, :] * mt[s - 1, b, r, :]))
 
@@ -406,7 +417,9 @@
     keep_out(0)
     start_pair(coef_up, coef_down)
     start_pair(halo_up(0), halo_down(0))
-    for c in [local[1]] + local[4:10]:
+    local[1].wait()
+    send_steps()
+    for c in local[4:10]:
         c.wait()
     stencil_plane()
     land_pair(coef_up, coef_down)
@@ -435,8 +448,9 @@
             out[b, x] = uh[4, b, x] - step * mh[4, b, x]
 
     for unit in range(SECTIONS):
-        wait_bytes(tb.at[unit, 0 : width(unit), 0 : (n - 1) * rows, :], ss.at[unit])
+        wait_bytes(tb.at[unit, 0:nv, 0 : (n - 1) * rows, :], ss.at[unit])
         wait_bytes(mt.at[unit, :, 0 : (n - 1) * rows, :], ss.at[SECTIONS + unit])
+    wait_bytes(tb.at[1, nv, 0 : (n - 1) * rows, :], ss.at[2 * SECTIONS])
     for s in range(SECTIONS):
         sent_pair(halo_up(s), halo_down(s))
     sent_pair(coef_up, coef_down)
@@ -473,8 +487,8 @@
             pltpu.SMEM((1,), f32),
             pltpu.SMEM((1,), f32),
             dma((12,)),
-            dma((2 * SECTIONS,)),
-            dma((SECTIONS,)),
+            dma((2 * SECTIONS + 1,)),
+            dma((SECTIONS + 1,)),
             dma((SECTIONS, lay)),
             dma((SECTIONS, 2)),
             dma((SECTIONS, 2)),

time: 48.8 us -> 47.7 us (0.977)
  Pallas kernels: 46.7 us -> 45.6 us
    pallas_call x1, Pallas kernels: 46.7 us -> 45.6 us  [on_device(): pl.pallas_call(functools.partial(kernel, n, cells), out_shape=pltpu.VMEM(...]
where the time goes in v5:
time: 47.7 us; the launch traced here: 47.6 us
  Pallas kernels  45.6 us (96%)
  between operations  1.3 us (3%)
  local copies, waits for them, and re-layouts  0.67 us (1%)
    pallas_call x1, Pallas kernels, on_device(): pl.pallas_call(functools.partial(kernel, n, cells), out_shape=pltpu.VMEM(...  45.6 us

profile of v5, /device:TPU:0, one launch (start us, length us, event | category | flops | bytes accessed | tf_op | source)
XLA Modules:
  0.0 47.6 jit_solution(9865911768140778126)
XLA Ops:
  1.3 45.6 %shard_map.82 = f32[5,4,16,128]{3,2,1,0:T(8,128)S(1)} custom-call(f32[5,4,16,128]{3,2,1,0:T(8,128)} %bitcast.9, f32[5,4,16,128]{3,2,1,0:T(8,128)} %bitcast.10, f32[3,5,5,4,16,128]{5,4,3,2,1,0:T(8,128)} %bitcast.8, f32[3,4,16,128]{3,2,1,0:T(8,128)} %bitcast.11, f32[3,4,16,128]{3,2,1,0:T(8,128)} %bitcast.12, f32[4,16,128]{2,1,0:T(8,128)} %bitcast.13, ...), custom_call_target="tpu_custom_call" | custom-call | tf_op jit(solution)/shard_map/pallas_call | solution.py:468
  46.9 0.7 %copy.10 = f32[1,5,4,16,128]{4,3,2,1,0:T(8,128)} copy(f32[1,5,4,16,128]{4,3,2,1,0:T(8,128)S(1)} %bitcast.7) | data formatting | bytes 327680

commit v6 on v5

--- a/solution.py
+++ b/solution.py
@@ -378,6 +378,18 @@
         def _(x):
             send_layer(s, x)
 
+    local[0].wait()
+    local[2].wait()
+    local[3].wait()
+    pl.semaphore_wait(barrier, n - 1 + lo + hi)
+
+    for p, (x, y) in zip(others, spots):
+        send_out(0, p, x, y)
+    keep_out(0)
+    start_pair(coef_up, coef_down)
+    start_pair(halo_up(0), halo_down(0))
+    local[1].wait()
+    send_steps()
     slope, curve = coupling_tables(n)
     part = lax.broadcasted_iota(jnp.int32, (TILE, nz), 0) // rows
     local[10].wait()
@@ -407,18 +419,6 @@
     def _():
         cx[:, 2 + lay :] = jnp.zeros((2, 2, ny, nz), jnp.float32)
 
-    local[0].wait()
-    local[2].wait()
-    local[3].wait()
-    pl.semaphore_wait(barrier, n - 1 + lo + hi)
-
-    for p, (x, y) in zip(others, spots):
-        send_out(0, p, x, y)
-    keep_out(0)
-    start_pair(coef_up, coef_down)
-    start_pair(halo_up(0), halo_down(0))
-    local[1].wait()
-    send_steps()
     for c in local[4:10]:
         c.wait()
     stencil_plane()

time: 47.7 us -> 47.7 us (level)
  no operation moved by 1% of the time
where the time goes in v6:
time: 47.7 us; the launch traced here: 47.6 us
  Pallas kernels  45.6 us (96%)
  between operations  1.3 us (3%)
  local copies, waits for them, and re-layouts  0.67 us (1%)
    pallas_call x1, Pallas kernels, on_device(): pl.pallas_call(functools.partial(kernel, n, cells), out_shape=pltpu.VMEM(...  45.6 us

profile of v6, /device:TPU:0, one launch (start us, length us, event | category | flops | bytes accessed | tf_op | source)
XLA Modules:
  0.0 47.6 jit_solution(659430215695850729)
XLA Ops:
  1.3 45.6 %shard_map.82 = f32[5,4,16,128]{3,2,1,0:T(8,128)S(1)} custom-call(f32[5,4,16,128]{3,2,1,0:T(8,128)} %bitcast.9, f32[5,4,16,128]{3,2,1,0:T(8,128)} %bitcast.10, f32[3,5,5,4,16,128]{5,4,3,2,1,0:T(8,128)} %bitcast.8, f32[3,4,16,128]{3,2,1,0:T(8,128)} %bitcast.11, f32[3,4,16,128]{3,2,1,0:T(8,128)} %bitcast.12, f32[4,16,128]{2,1,0:T(8,128)} %bitcast.13, ...), custom_call_target="tpu_custom_call" | custom-call | tf_op jit(solution)/shard_map/pallas_call | solution.py:468
  46.9 0.7 %copy.10 = f32[1,5,4,16,128]{4,3,2,1,0:T(8,128)} copy(f32[1,5,4,16,128]{4,3,2,1,0:T(8,128)S(1)} %bitcast.7) | data formatting | bytes 327680
